TPU v7x, 512 devices: a whole 4x8x8 slice. The times are simulated.
512 devices in a mesh: tok: 8 (over z), wid: 64 (over x, y, core).
Axes of the slice: x: 4, y: 8, z: 8, core: 2. Of those that a mesh axis runs over, the one named last changes fastest.
Arguments:
- tokens: bfloat16 [1536, 4096], P('tok', 'wid'), may hold values from -80 to 80
- gate_a: bfloat16 [16384, 4096], P('wid', 'tok'), may hold values from -0.09375 to 0.09375
- up_a: bfloat16 [16384, 4096], P('wid', 'tok'), may hold values from -0.09375 to 0.09375
- gate_b: bfloat16 [16384, 4096], P('wid', 'tok'), may hold values from -0.09375 to 0.09375
- up_b: bfloat16 [16384, 4096], P('wid', 'tok'), may hold values from -0.09375 to 0.09375
- down_a: bfloat16 [16384, 4096], P('wid', 'tok'), may hold values from -0.125 to 0.125
- down_b: bfloat16 [16384, 4096], P('wid', 'tok'), may hold values from -0.125 to 0.125
- block_perm: int32 [128], replicated, may hold values from 0 to 127, each once
Outputs:
- merged: bfloat16 [1536, 4096], P('tok', 'wid')
Inputs may be any that keep to these rules, and one draw needn't show every extreme that they name: block_perm names every block number once.
All inputs are finite; a program needn't handle non-finite values.
Results may differ from a plain program's by a relative error of at most 0.0058.
Values may be sent and summed in bfloat16 or wider, within the bound.
A program may use at most 64 MiB of HBM per device.

v0:
```python
import jax
import jax.numpy as jnp
from jax import lax
from jax.sharding import PartitionSpec as P

FF = 16384
BLOCK = 128


def sigmoid_linear(preact):
    return preact / (1.0 + jnp.exp(-preact))


def reorder_blocks(matrix_in, block_perm):
    shaped = matrix_in.reshape(FF // BLOCK, BLOCK, matrix_in.shape[1])
    return jnp.take(shaped, block_perm, axis=0).reshape(matrix_in.shape)


def add_products(pieces, gathered):
    return tuple(
        (
            lax.dot_general(
                gathered, piece, (((1,), (1,)), ((), ())), preferred_element_type=jnp.float32
            )
            for piece in pieces
        )
    )


def local(tokens, gate_a, up_a, gate_b, up_b, down_a, down_b, block_perm):
    gathered = lax.all_gather(tokens, "wid", axis=1, tiled=True)
    row_count = gathered.shape[0]
    shipped = (
        lax.all_to_all(gate_b, "wid", split_axis=1, concat_axis=0, tiled=True),
        lax.all_to_all(up_b, "wid", split_axis=1, concat_axis=0, tiled=True),
        lax.all_to_all(down_b, "wid", split_axis=1, concat_axis=0, tiled=True),
    )
    gate_src, up_src, down_perm = (
        lax.all_to_all(
            reorder_blocks(shipped[0], block_perm), "wid", split_axis=0, concat_axis=1, tiled=True
        ),
        lax.all_to_all(
            reorder_blocks(shipped[1], block_perm), "wid", split_axis=0, concat_axis=1, tiled=True
        ),
        lax.all_to_all(
            reorder_blocks(shipped[2], block_perm), "wid", split_axis=0, concat_axis=1, tiled=True
        ),
    )
    gate_av, up_av, gate_bv, up_bv = add_products(
        (
            lax.all_gather(gate_a, "tok", axis=1, tiled=True),
            lax.all_gather(up_a, "tok", axis=1, tiled=True),
            lax.all_gather(gate_src, "tok", axis=1, tiled=True),
            lax.all_gather(up_src, "tok", axis=1, tiled=True),
        ),
        gathered,
    )
    hid_a = sigmoid_linear(gate_av) * up_av
    hid_b = sigmoid_linear(gate_bv) * up_bv
    hid_m = sigmoid_linear(0.5 * (gate_av + gate_bv)) * (0.5 * (up_av + up_bv))
    token_total = row_count * lax.axis_size("tok")
    totals = lax.psum(
        (jnp.sum(hid_a, axis=0), jnp.sum(hid_b, axis=0), jnp.sum(hid_m, axis=0)), "tok"
    )
    centers = tuple((total / token_total for total in totals))
    squares = lax.psum(
        (
            jnp.sum((hid_a - centers[0]) ** 2, axis=0),
            jnp.sum((hid_b - centers[1]) ** 2, axis=0),
            jnp.sum((hid_m - centers[2]) ** 2, axis=0),
        ),
        "tok",
    )
    spreads = tuple((square / token_total for square in squares))
    deviations = tuple((jnp.sqrt(spread + 1e-05) for spread in spreads))
    target_std = 0.5 * (deviations[0] + deviations[1])
    target_mean = 0.5 * (centers[0] + centers[1])
    repaired = ((hid_m - centers[2]) / deviations[2] * target_std + target_mean).astype(
        jnp.bfloat16
    )
    down_mid = ((down_a.astype(jnp.float32) + down_perm.astype(jnp.float32)) * 0.5).astype(
        jnp.bfloat16
    )
    partial_out = jnp.dot(
        repaired,
        lax.all_gather(down_mid, "tok", axis=1, tiled=True),
        preferred_element_type=jnp.float32,
    )
    summed = lax.psum_scatter(partial_out, "wid", scatter_dimension=1, tiled=True)
    return summed.astype(jnp.bfloat16)


def solution(mesh):
    return jax.shard_map(
        local,
        mesh=mesh,
        in_specs=(
            P("tok", "wid"),
            P("wid", "tok"),
            P("wid", "tok"),
            P("wid", "tok"),
            P("wid", "tok"),
            P("wid", "tok"),
            P("wid", "tok"),
            P(),
        ),
        out_specs=P("tok", "wid"),
        check_vma=False,
    )
```

profile of v0, /device:TPU:16, one launch (start us, length us, event | category | flops | bytes accessed | tf_op | source)
XLA Modules:
  0.0 485.1 jit_solution(15461387688074729571)
XLA Ops:
  6.5 0.0 copy-start.1
  6.5 0.0 copy-start.3
  6.5 0.0 all-gather.7.cloned.1.call-start
  6.5 0.7 all-gather.7.cloned.1.call-update
  7.3 0.0 all-gather.9.cloned.1.call-start
  7.3 0.7 all-gather.9.cloned.1.call-update
  8.0 0.0 all-gather.13.cloned.1.call-start
  8.1 0.7 all-gather.13.cloned.1.call-update
  8.7 1.8 copy.9
  10.5 10.5 %all-to-all-start = ((bf16[256,64,8]{0,2,1:T(8,128)(2,1)}), bf16[256,64,8]{0,2,1:T(8,128)(2,1)S(1)}, u32[]{:S(2)}, u32[]{:S(2)}) async-start(bf16[256,64,8]{0,2,1:T(8,128)(2,1)} %bitcast), calls=%async_computation | async-start | bytes 524288 | tf_op jit(solution)/shard_map/all_to_all | solution.py:34
  21.0 1.8 copy.10
  22.8 9.9 %all-to-all-done = bf16[256,64,8]{0,2,1:T(8,128)(2,1)S(1)} async-done(((bf16[256,64,8]{0,2,1:T(8,128)(2,1)}), bf16[256,64,8]{0,2,1:T(8,128)(2,1)S(1)}, u32[]{:S(2)}, u32[]{:S(2)}) %all-to-all-start) | async-done | bytes 262176 | tf_op jit(solution)/shard_map/all_to_all | solution.py:34
  32.7 6.3 %all-to-all-start.2 = ((bf16[256,64,8]{0,2,1:T(8,128)(2,1)}), bf16[256,64,8]{0,2,1:T(8,128)(2,1)S(1)}, u32[]{:S(2)}, u32[]{:S(2)}) async-start(bf16[256,64,8]{0,2,1:T(8,128)(2,1)} %bitcast.7), calls=%async_computation.2 | async-start | bytes 524288 | tf_op jit(solution)/shard_map/all_to_all | solution.py:35
  39.0 0.0 copy-done.1
  39.0 0.8 copy.12
  39.9 10.8 %all-to-all-done.2 = bf16[256,64,8]{0,2,1:T(8,128)(2,1)S(1)} async-done(((bf16[256,64,8]{0,2,1:T(8,128)(2,1)}), bf16[256,64,8]{0,2,1:T(8,128)(2,1)S(1)}, u32[]{:S(2)}, u32[]{:S(2)}) %all-to-all-start.2) | async-done | bytes 262176 | tf_op jit(solution)/shard_map/all_to_all | solution.py:35
  50.7 6.7 %all-to-all-start.4 = ((bf16[256,64,8]{0,2,1:T(8,128)(2,1)}), bf16[256,64,8]{0,2,1:T(8,128)(2,1)S(1)}, u32[]{:S(2)}, u32[]{:S(2)}) async-start(bf16[256,64,8]{0,2,1:T(8,128)(2,1)} %bitcast.14), calls=%async_computation.4 | async-start | bytes 524288 | tf_op jit(solution)/shard_map/all_to_all | solution.py:36
  57.4 0.0 all-gather.11.cloned.1.call-start
  57.5 0.0 copy-done.3
  57.5 0.7 gather_fusion
  58.2 0.7 gather_fusion.1
  58.9 10.2 %all-to-all-done.4 = bf16[256,64,8]{0,2,1:T(8,128)(2,1)S(1)} async-done(((bf16[256,64,8]{0,2,1:T(8,128)(2,1)}), bf16[256,64,8]{0,2,1:T(8,128)(2,1)S(1)}, u32[]{:S(2)}, u32[]{:S(2)}) %all-to-all-start.4) | async-done | bytes 262176 | tf_op jit(solution)/shard_map/all_to_all | solution.py:36
  69.1 0.7 gather_fusion.2
  69.8 0.0 copy-start.2
  69.8 0.9 broadcast_select_fusion.2
  70.8 19.1 %all_to_all.99 = bf16[64,256,8]{1,2,0:T(8,128)(2,1)} all-to-all(bf16[64,256,8]{1,2,0:T(8,128)(2,1)S(1)} %bitcast.48), channel_id=1, replica_groups=mesh['tok'=8,'wid'=64] {'wid'}, dimensions={0} | all-to-all | bytes 524288 | tf_op jit(solution)/shard_map/all_to_all | solution.py:39
  89.8 0.0 all-gather.11.cloned.1.call-update
  89.8 0.0 all-gather.15.cloned.1.call-start
  89.9 18.3 %all_to_all.100 = bf16[64,256,8]{1,2,0:T(8,128)(2,1)} all-to-all(bf16[64,256,8]{1,2,0:T(8,128)(2,1)S(1)} %bitcast.47), channel_id=1, replica_groups=mesh['tok'=8,'wid'=64] {'wid'}, dimensions={0} | all-to-all | bytes 524288 | tf_op jit(solution)/shard_map/all_to_all | solution.py:42
  108.2 0.0 all-gather.15.cloned.1.call-update
  108.2 6.3 %all-to-all-start.5 = ((bf16[64,256,8]{1,2,0:T(8,128)(2,1)}), bf16[64,256,8]{1,2,0:T(8,128)(2,1)S(1)}, u32[]{:S(2)}, u32[]{:S(2)}) async-start(bf16[64,256,8]{1,2,0:T(8,128)(2,1)} %bitcast.17), calls=%async_computation.5 | async-start | bytes 524288 | tf_op jit(solution)/shard_map/all_to_all | solution.py:45
  114.6 0.0 all-gather.17.cloned.1.call-start
  114.6 0.0 copy-done.2
  114.6 0.1 copy.11
  114.8 11.5 %all-to-all-done.5 = bf16[64,256,8]{1,2,0:T(8,128)(2,1)S(1)} async-done(((bf16[64,256,8]{1,2,0:T(8,128)(2,1)}), bf16[64,256,8]{1,2,0:T(8,128)(2,1)S(1)}, u32[]{:S(2)}, u32[]{:S(2)}) %all-to-all-start.5) | async-done | bytes 262176 | tf_op jit(solution)/shard_map/all_to_all | solution.py:45
  126.3 0.8 fusion.1
  127.1 0.0 all-gather.17.cloned.1.call-update
  127.1 0.0 reduce-scatter.2.cloned.1.call-start
  127.2 0.0 all-gather.7.cloned.1.call-done
  127.2 0.0 copy-start
  127.2 16.2 %all-gather.9.cloned.1.call-done = bf16[256,4096]{1,0:T(8,128)(2,1)} async-done(((bf16[256,512]{1,0:T(8,128)(2,1)}), bf16[256,4096]{1,0:T(8,128)(2,1)}) %all-gather.9.cloned.1.call-update) | async-done | bytes 2097168 | tf_op jit(solution)/shard_map/all_gather | solution.py:51
  143.4 3.1 fusion.10
  146.4 41.8 %all-gather.13.cloned.1.call-done = bf16[256,4096]{1,0:T(8,128)(2,1)} async-done(((bf16[256,512]{1,0:T(8,128)(2,1)}), bf16[256,4096]{1,0:T(8,128)(2,1)}) %all-gather.13.cloned.1.call-update) | async-done | bytes 2097168 | tf_op jit(solution)/shard_map/all_gather | solution.py:52
  188.2 0.0 copy-done
  188.2 2.4 fusion.11
  190.7 42.3 %all-gather.11.cloned.1.call-done = bf16[256,4096]{0,1:T(8,128)(2,1)} async-done(((bf16[256,512]{0,1:T(8,128)(2,1)}), bf16[256,4096]{0,1:T(8,128)(2,1)}) %all-gather.11.cloned.1.call-update) | async-done | bytes 2097168 | tf_op jit(solution)/shard_map/all_gather | solution.py:53
  232.9 2.4 convolution_bitcast_fusion.1
  235.4 42.2 %all-gather.15.cloned.1.call-done = bf16[256,4096]{0,1:T(8,128)(2,1)} async-done(((bf16[256,512]{0,1:T(8,128)(2,1)}), bf16[256,4096]{0,1:T(8,128)(2,1)}) %all-gather.15.cloned.1.call-update) | async-done | bytes 2097168 | tf_op jit(solution)/shard_map/all_gather | solution.py:54
  277.6 2.5 fusion.8
  280.1 15.7 %all-reduce.1 = (f32[256]{0:T(256)S(1)}, f32[256]{0:T(256)S(1)}, f32[256]{0:T(256)S(1)}) all-reduce(f32[256]{0:T(256)S(1)} %get-tuple-element.20, f32[256]{0:T(256)S(1)} %get-tuple-element.14, f32[256]{0:T(256)S(1)} %get-tuple-element.18), channel_id=1, replica_groups=mesh['tok'=8,'wid'=64] {'tok'}, use_global_device_ids=true, to_apply=%region_5.7 | all-reduce | flops 768 | bytes 6144 | tf_op jit(solution)/shard_map/psum | solution.py:62
  295.9 0.1 multiply_reduce_fusion
  295.9 14.7 %all-reduce = (f32[256]{0:T(256)S(1)}, f32[256]{0:T(256)S(1)}, f32[256]{0:T(256)S(1)}) all-reduce(f32[256]{0:T(256)S(1)} %get-tuple-element.28, f32[256]{0:T(256)S(1)} %get-tuple-element.29, f32[256]{0:T(256)S(1)} %multiply_reduce_fusion.2), channel_id=1, replica_groups=mesh['tok'=8,'wid'=64] {'tok'}, use_global_device_ids=true, to_apply=%region_11.13 | all-reduce | flops 768 | bytes 6144 | tf_op jit(solution)/shard_map/psum | solution.py:66
  310.7 11.2 %all-gather.17.cloned.1.call-done = bf16[256,4096]{0,1:T(8,128)(2,1)} async-done(((bf16[256,512]{0,1:T(8,128)(2,1)}), bf16[256,4096]{0,1:T(8,128)(2,1)}) %all-gather.17.cloned.1.call-update) | async-done | bytes 2097168 | tf_op jit(solution)/shard_map/all_gather | solution.py:86
  321.9 4.3 fusion.2
  326.2 0.0 reduce-scatter.2.cloned.1.call-update
  326.2 150.6 %reduce-scatter.2.cloned.1.call-done = f32[192,64]{0,1:T(8,128)} async-done(((f32[192,4096]{0,1:T(8,128)}), f32[192,64]{0,1:T(8,128)}) %reduce-scatter.2.cloned.1.call-update) | async-done | bytes 49168 | tf_op jit(solution)/shard_map/reduce_scatter | solution.py:89
  476.8 1.5 convert_element_type.27
  (8 shorter events, 0.1 us)
Async XLA Ops:
  6.5 32.5 %copy-start.1 = (bf16[256,512]{1,0:T(8,128)(2,1)S(1)}, bf16[256,512]{1,0:T(8,128)(2,1)}, u32[]{:S(2)}) copy-start(bf16[256,512]{1,0:T(8,128)(2,1)} %param.16) | copy-start | bytes 786436
  6.5 50.9 %copy-start.3 = (s32[128]{0:T(128)S(1)}, s32[128]{0:T(128)}, u32[]{:S(2)}) copy-start(s32[128]{0:T(128)} %param.17) | copy-start | bytes 1540
  6.5 120.6 %all-gather.7.cloned.1.call-start = ((), (), s32[]{:S(2)}) async-start(), calls=%async_computation.7 | async-start | bytes 2129920 | tf_op jit(solution)/shard_map/all_gather | solution.py:31
  7.3 136.1 %all-gather.9.cloned.1.call-start = ((), (), s32[]{:S(2)}) async-start(), calls=%async_computation.8 | async-start | bytes 2359296 | tf_op jit(solution)/shard_map/all_gather | solution.py:51
  8.0 180.2 %all-gather.13.cloned.1.call-start = ((), (), s32[]{:S(2)}) async-start(), calls=%async_computation.10 | async-start | bytes 2359296 | tf_op jit(solution)/shard_map/all_gather | solution.py:52
  10.5 22.2 %all-to-all-start = ((bf16[256,64,8]{0,2,1:T(8,128)(2,1)}), bf16[256,64,8]{0,2,1:T(8,128)(2,1)S(1)}, u32[]{:S(2)}, u32[]{:S(2)}) async-start(bf16[256,64,8]{0,2,1:T(8,128)(2,1)} %bitcast), calls=%async_computation | async-start | bytes 524288 | tf_op jit(solution)/shard_map/all_to_all | solution.py:34
  32.7 18.0 %all-to-all-start.2 = ((bf16[256,64,8]{0,2,1:T(8,128)(2,1)}), bf16[256,64,8]{0,2,1:T(8,128)(2,1)S(1)}, u32[]{:S(2)}, u32[]{:S(2)}) async-start(bf16[256,64,8]{0,2,1:T(8,128)(2,1)} %bitcast.7), calls=%async_computation.2 | async-start | bytes 524288 | tf_op jit(solution)/shard_map/all_to_all | solution.py:35
  50.7 18.4 %all-to-all-start.4 = ((bf16[256,64,8]{0,2,1:T(8,128)(2,1)}), bf16[256,64,8]{0,2,1:T(8,128)(2,1)S(1)}, u32[]{:S(2)}, u32[]{:S(2)}) async-start(bf16[256,64,8]{0,2,1:T(8,128)(2,1)} %bitcast.14), calls=%async_computation.4 | async-start | bytes 524288 | tf_op jit(solution)/shard_map/all_to_all | solution.py:36
  57.4 175.5 %all-gather.11.cloned.1.call-start = ((), (), s32[]{:S(2)}) async-start(), calls=%async_computation.9 | async-start | bytes 2359296 | tf_op jit(solution)/shard_map/all_gather | solution.py:53
  69.8 44.8 %copy-start.2 = (bf16[256,512]{1,0:T(8,128)(2,1)S(1)}, bf16[256,512]{1,0:T(8,128)(2,1)}, u32[]{:S(2)}) copy-start(bf16[256,512]{1,0:T(8,128)(2,1)} %param.15) | copy-start | bytes 786436
  89.8 187.7 %all-gather.15.cloned.1.call-start = ((), (), s32[]{:S(2)}) async-start(), calls=%async_computation.11 | async-start | bytes 2359296 | tf_op jit(solution)/shard_map/all_gather | solution.py:54
  108.2 18.0 %all-to-all-start.5 = ((bf16[64,256,8]{1,2,0:T(8,128)(2,1)}), bf16[64,256,8]{1,2,0:T(8,128)(2,1)S(1)}, u32[]{:S(2)}, u32[]{:S(2)}) async-start(bf16[64,256,8]{1,2,0:T(8,128)(2,1)} %bitcast.17), calls=%async_computation.5 | async-start | bytes 524288 | tf_op jit(solution)/shard_map/all_to_all | solution.py:45
  114.6 207.3 %all-gather.17.cloned.1.call-start = ((), (), s32[]{:S(2)}) async-start(), calls=%async_computation.12 | async-start | bytes 2359296 | tf_op jit(solution)/shard_map/all_gather | solution.py:86
  127.1 349.7 %reduce-scatter.2.cloned.1.call-start = ((), (), s32[]{:S(2)}) async-start(), calls=%async_computation.13 | async-start | bytes 4259840 | tf_op jit(solution)/shard_map/reduce_scatter | solution.py:89
  127.2 61.0 %copy-start = (bf16[192,4096]{0,1:T(8,128)(2,1)S(1)}, bf16[192,4096]{0,1:T(8,128)(2,1)}, u32[]{:S(2)}) copy-start(bf16[192,4096]{0,1:T(8,128)(2,1)} %all-gather.7.cloned.1.call-done) | copy-start | bytes 4718596
Sparse Core Ops, SparseCore 0:
  10.7 88.4 all-gather.6
  101.3 41.9 all-gather.8
  145.4 42.7 all-gather.12
  190.2 42.7 all-gather.10
  234.8 42.7 all-gather.14
  279.5 42.3 all-gather.16
  326.6 150.1 reduce-scatter.1
where the time goes:
time: 486 us; the launch traced here: 485 us
  waiting for transfers between devices  349 us (72%)
  blocking collectives  67.8 us (14%)
  starting transfers between devices  30 us (6%)
  matrix products  14.7 us (3%)
  between operations  13.6 us (3%)
  local copies, waits for them, and re-layouts  6.63 us (1%)
    reduce_scatter x1, waiting for transfers between devices, local(): lax.psum_scatter(partial_out, 'wid', scatter_dimension=1, tiled=True)  151 us
    all_gather x1, waiting for transfers between devices, local(): lax.all_gather(gate_src, 'tok', axis=1, tiled=True)  42.3 us
    all_gather x1, waiting for transfers between devices, local(): lax.all_gather(up_src, 'tok', axis=1, tiled=True)  42.2 us
    all_gather x1, waiting for transfers between devices, local(): lax.all_gather(up_a, 'tok', axis=1, tiled=True)  41.8 us
    all_to_all x1, blocking collectives, local(): lax.all_to_all(reorder_blocks(shipped[0], block_perm), 'wid', split_axis=...  19.1 us
    all_to_all x1, blocking collectives, local(): lax.all_to_all(reorder_blocks(shipped[1], block_perm), 'wid', split_axis=...  18.3 us
    all_gather x1, waiting for transfers between devices, local(): lax.all_gather(gate_a, 'tok', axis=1, tiled=True)  16.2 us
    psum x1, blocking collectives, local(): lax.psum((jnp.sum(hid_a, axis=0), jnp.sum(hid_b, axis=0), jnp.sum(hid_m,...  15.7 us
  transfers between devices with their start and end apart: 11, of which 10 were waited for; matrix products, arithmetic and copies ran while one was open for 4% of the time, Pallas kernels for 0%

commit v1 on v0

--- a/solution.py
+++ b/solution.py
@@ -1,3 +1,4 @@
+import functools
 import jax
 import jax.numpy as jnp
 from jax import lax
@@ -5,6 +6,21 @@
 
 FF = 16384
 BLOCK = 128
+
+
+def pack_quotas(u_in, lane_axis):
+    return jnp.concatenate(
+        jax.lax.all_to_all(
+            jnp.stack(jnp.split(u_in, jax.lax.axis_size(lane_axis), axis=1)),
+            axis_name=lane_axis,
+            concat_axis=0,
+            split_axis=0,
+        ),
+        axis=0,
+    )
+
+
+clear_sections_up = functools.partial(pack_quotas, lane_axis="wid")
 
 
 def sigmoid_linear(preact):
@@ -31,7 +47,7 @@
     gathered = lax.all_gather(tokens, "wid", axis=1, tiled=True)
     row_count = gathered.shape[0]
     shipped = (
-        lax.all_to_all(gate_b, "wid", split_axis=1, concat_axis=0, tiled=True),
+        clear_sections_up(gate_b),
         lax.all_to_all(up_b, "wid", split_axis=1, concat_axis=0, tiled=True),
         lax.all_to_all(down_b, "wid", split_axis=1, concat_axis=0, tiled=True),
     )

time: 486 us -> 487 us (level)
  local copies, waits for them, and re-layouts: 6.63 us -> 62.2 us
  waiting for transfers between devices: 349 us -> 294 us
    unnamed x12 -> x142, local copies, waits for them, and re-layouts: 4.56 us -> 55.9 us
    all_gather x1, waiting for transfers between devices: 41.8 us -> 0.99 us  [local(): lax.all_gather(up_a, 'tok', axis=1, tiled=True)]
    all_gather x1, waiting for transfers between devices: 16.2 us -> 0.02 us  [local(): lax.all_gather(gate_a, 'tok', axis=1, tiled=True)]
  transfers between devices with their start and end apart: 11 -> 11, of which waited for: 10 -> 9; matrix products, arithmetic and copies ran while one was open for 4% -> 15% of each run, Pallas kernels for 0% -> 0%
where the time goes in v1:
time: 487 us; the launch traced here: 485 us
  waiting for transfers between devices  294 us (60%)
  blocking collectives  66.3 us (14%)
  local copies, waits for them, and re-layouts  62.2 us (13%)
  starting transfers between devices  30.4 us (6%)
  matrix products  14.9 us (3%)
  between operations  13.8 us (3%)
    reduce_scatter x1, waiting for transfers between devices, local(): lax.psum_scatter(partial_out, 'wid', scatter_dimension=1, tiled=True)  151 us
    unnamed x142, local copies, waits for them, and re-layouts  55.9 us
    all_gather x1, waiting for transfers between devices, local(): lax.all_gather(gate_src, 'tok', axis=1, tiled=True)  42.7 us
    all_gather x1, waiting for transfers between devices, local(): lax.all_gather(up_src, 'tok', axis=1, tiled=True)  42.2 us
    all_to_all x1, blocking collectives, local(): lax.all_to_all(reorder_blocks(shipped[1], block_perm), 'wid', split_axis=...  17.9 us
    all_to_all x1, blocking collectives, local(): lax.all_to_all(reorder_blocks(shipped[0], block_perm), 'wid', split_axis=...  17.9 us
    psum x1, blocking collectives, local(): lax.psum((jnp.sum(hid_a, axis=0), jnp.sum(hid_b, axis=0), jnp.sum(hid_m,...  15.7 us
    psum x1, blocking collectives, local(): lax.psum((jnp.sum((hid_a - centers[0]) ** 2, axis=0), jnp.sum((hid_b - ce...  14.7 us
  transfers between devices with their start and end apart: 11, of which 9 were waited for; matrix products, arithmetic and copies ran while one was open for 15% of the time, Pallas kernels for 0%

profile of v1, /device:TPU:16, one launch (start us, length us, event | category | flops | bytes accessed | tf_op | source)
XLA Modules:
  0.0 485.2 jit_solution(18330942170350124329)
XLA Ops:
  6.5 0.7 all-gather.7.cloned.1.call-update
  7.3 0.7 all-gather.9.cloned.1.call-update
  8.1 0.7 all-gather.13.cloned.1.call-update
  8.7 1.6 fusion.13
  10.3 1.3 fusion.12
  12.5 0.6 constant_dynamic-update-slice_fusion.63
  13.6 0.9 copy.92
  14.5 0.9 copy.93
  15.4 0.9 copy.94
  16.3 0.9 copy.95
  17.2 0.9 copy.96
  18.1 0.9 copy.97
  19.0 0.9 copy.98
  19.9 0.9 copy.99
  20.9 0.9 copy.100
  21.8 0.9 copy.101
  22.7 0.9 copy.102
  23.6 0.9 copy.103
  24.5 0.9 copy.104
  25.4 1.0 copy.105
  29.9 0.6 constant_dynamic-update-slice_fusion.62
  31.1 0.6 constant_dynamic-update-slice_fusion.60
  34.7 0.6 constant_dynamic-update-slice_fusion.54
  39.4 0.6 constant_dynamic-update-slice_fusion.46
  40.6 0.6 constant_dynamic-update-slice_fusion.44
  44.7 0.6 constant_dynamic-update-slice_fusion.37
  45.3 0.6 constant_dynamic-update-slice_fusion.36
  47.1 0.6 constant_dynamic-update-slice_fusion.33
  47.6 0.6 constant_dynamic-update-slice_fusion.32
  52.4 0.6 constant_dynamic-update-slice_fusion.24
  53.6 0.6 constant_dynamic-update-slice_fusion.22
  55.3 0.6 constant_dynamic-update-slice_fusion.19
  63.0 0.6 constant_dynamic-update-slice_fusion.6
  66.6 0.6 constant_dynamic-update-slice_fusion
  67.1 10.5 %all-to-all-start = ((bf16[64,256,8]{1,2,0:T(8,128)(2,1)}), bf16[64,256,8]{1,2,0:T(8,128)(2,1)S(1)}, u32[]{:S(2)}, u32[]{:S(2)}) async-start(bf16[64,256,8]{1,2,0:T(8,128)(2,1)} %constant_dynamic-update-slice_fusion), calls=%async_computation | async-start | bytes 524288 | tf_op jit(solution)/shard_map/all_to_all | solution.py:13
  77.6 0.9 copy.82
  78.5 11.8 %all-to-all-done = bf16[64,256,8]{1,2,0:T(8,128)(2,1)S(1)} async-done(((bf16[64,256,8]{1,2,0:T(8,128)(2,1)}), bf16[64,256,8]{1,2,0:T(8,128)(2,1)S(1)}, u32[]{:S(2)}, u32[]{:S(2)}) %all-to-all-start) | async-done | bytes 262176 | tf_op jit(solution)/shard_map/all_to_all | solution.py:13
  90.2 6.9 %all-to-all-start.2 = ((bf16[256,64,8]{0,2,1:T(8,128)(2,1)}), bf16[256,64,8]{0,2,1:T(8,128)(2,1)S(1)}, u32[]{:S(2)}, u32[]{:S(2)}) async-start(bf16[256,64,8]{0,2,1:T(8,128)(2,1)} %bitcast.69), calls=%async_computation.2 | async-start | bytes 524288 | tf_op jit(solution)/shard_map/all_to_all | solution.py:51
  97.1 0.8 copy.84
  98.0 10.9 %all-to-all-done.2 = bf16[256,64,8]{0,2,1:T(8,128)(2,1)S(1)} async-done(((bf16[256,64,8]{0,2,1:T(8,128)(2,1)}), bf16[256,64,8]{0,2,1:T(8,128)(2,1)S(1)}, u32[]{:S(2)}, u32[]{:S(2)}) %all-to-all-start.2) | async-done | bytes 262176 | tf_op jit(solution)/shard_map/all_to_all | solution.py:51
  108.8 6.3 %all-to-all-start.4 = ((bf16[256,64,8]{0,2,1:T(8,128)(2,1)}), bf16[256,64,8]{0,2,1:T(8,128)(2,1)S(1)}, u32[]{:S(2)}, u32[]{:S(2)}) async-start(bf16[256,64,8]{0,2,1:T(8,128)(2,1)} %bitcast.76), calls=%async_computation.4 | async-start | bytes 524288 | tf_op jit(solution)/shard_map/all_to_all | solution.py:52
  115.3 0.7 gather_fusion
  115.9 0.7 gather_fusion.1
  116.6 10.2 %all-to-all-done.4 = bf16[256,64,8]{0,2,1:T(8,128)(2,1)S(1)} async-done(((bf16[256,64,8]{0,2,1:T(8,128)(2,1)}), bf16[256,64,8]{0,2,1:T(8,128)(2,1)S(1)}, u32[]{:S(2)}, u32[]{:S(2)}) %all-to-all-start.4) | async-done | bytes 262176 | tf_op jit(solution)/shard_map/all_to_all | solution.py:52
  126.9 0.7 gather_fusion.2
  127.6 0.9 broadcast_select_fusion.2
  128.5 17.9 %all_to_all.88 = bf16[64,256,8]{1,2,0:T(8,128)(2,1)} all-to-all(bf16[64,256,8]{1,2,0:T(8,128)(2,1)S(1)} %bitcast.173), channel_id=1, replica_groups=mesh['tok'=8,'wid'=64] {'wid'}, dimensions={0} | all-to-all | bytes 524288 | tf_op jit(solution)/shard_map/all_to_all | solution.py:55
  146.5 17.9 %all_to_all.89 = bf16[64,256,8]{1,2,0:T(8,128)(2,1)} all-to-all(bf16[64,256,8]{1,2,0:T(8,128)(2,1)S(1)} %bitcast.172), channel_id=1, replica_groups=mesh['tok'=8,'wid'=64] {'wid'}, dimensions={0} | all-to-all | bytes 524288 | tf_op jit(solution)/shard_map/all_to_all | solution.py:58
  164.5 6.3 %all-to-all-start.5 = ((bf16[64,256,8]{1,2,0:T(8,128)(2,1)}), bf16[64,256,8]{1,2,0:T(8,128)(2,1)S(1)}, u32[]{:S(2)}, u32[]{:S(2)}) async-start(bf16[64,256,8]{1,2,0:T(8,128)(2,1)} %bitcast.79), calls=%async_computation.5 | async-start | bytes 524288 | tf_op jit(solution)/shard_map/all_to_all | solution.py:61
  171.0 11.5 %all-to-all-done.5 = bf16[64,256,8]{1,2,0:T(8,128)(2,1)S(1)} async-done(((bf16[64,256,8]{1,2,0:T(8,128)(2,1)}), bf16[64,256,8]{1,2,0:T(8,128)(2,1)S(1)}, u32[]{:S(2)}, u32[]{:S(2)}) %all-to-all-start.5) | async-done | bytes 262176 | tf_op jit(solution)/shard_map/all_to_all | solution.py:61
  182.5 0.8 fusion.1
  183.6 3.2 fusion.14
  186.9 1.0 all-gather.13.cloned.1.call-done
  187.9 2.4 fusion.15
  190.3 42.7 %all-gather.11.cloned.1.call-done = bf16[256,4096]{0,1:T(8,128)(2,1)} async-done(((bf16[256,512]{0,1:T(8,128)(2,1)}), bf16[256,4096]{0,1:T(8,128)(2,1)}) %all-gather.11.cloned.1.call-update) | async-done | bytes 2097168 | tf_op jit(solution)/shard_map/all_gather | solution.py:69
  233.0 2.4 convolution_bitcast_fusion.1
  235.5 42.2 %all-gather.15.cloned.1.call-done = bf16[256,4096]{0,1:T(8,128)(2,1)} async-done(((bf16[256,512]{0,1:T(8,128)(2,1)}), bf16[256,4096]{0,1:T(8,128)(2,1)}) %all-gather.15.cloned.1.call-update) | async-done | bytes 2097168 | tf_op jit(solution)/shard_map/all_gather | solution.py:70
  277.7 2.5 fusion.8
  280.3 15.7 %all-reduce.1 = (f32[256]{0:T(256)S(1)}, f32[256]{0:T(256)S(1)}, f32[256]{0:T(256)S(1)}) all-reduce(f32[256]{0:T(256)S(1)} %get-tuple-element.20, f32[256]{0:T(256)S(1)} %get-tuple-element.14, f32[256]{0:T(256)S(1)} %get-tuple-element.18), channel_id=1, replica_groups=mesh['tok'=8,'wid'=64] {'tok'}, use_global_device_ids=true, to_apply=%region_5.7 | all-reduce | flops 768 | bytes 6144 | tf_op jit(solution)/shard_map/psum | solution.py:78
  296.1 14.7 %all-reduce = (f32[256]{0:T(256)S(1)}, f32[256]{0:T(256)S(1)}, f32[256]{0:T(256)S(1)}) all-reduce(f32[256]{0:T(256)S(1)} %get-tuple-element.92, f32[256]{0:T(256)S(1)} %get-tuple-element.93, f32[256]{0:T(256)S(1)} %multiply_reduce_fusion.2), channel_id=1, replica_groups=mesh['tok'=8,'wid'=64] {'tok'}, use_global_device_ids=true, to_apply=%region_11.13 | all-reduce | flops 768 | bytes 6144 | tf_op jit(solution)/shard_map/psum | solution.py:82
  310.8 11.2 %all-gather.17.cloned.1.call-done = bf16[256,4096]{0,1:T(8,128)(2,1)} async-done(((bf16[256,512]{0,1:T(8,128)(2,1)}), bf16[256,4096]{0,1:T(8,128)(2,1)}) %all-gather.17.cloned.1.call-update) | async-done | bytes 2097168 | tf_op jit(solution)/shard_map/all_gather | solution.py:102
  322.0 4.3 fusion.2
  326.3 150.6 %reduce-scatter.2.cloned.1.call-done = f32[192,64]{0,1:T(8,128)} async-done(((f32[192,4096]{0,1:T(8,128)}), f32[192,64]{0,1:T(8,128)}) %reduce-scatter.2.cloned.1.call-update) | async-done | bytes 49168 | tf_op jit(solution)/shard_map/reduce_scatter | solution.py:105
  476.9 1.5 convert_element_type.27
  (136 shorter events, 34.5 us)
Async XLA Ops:
  6.5 3.8 copy-start
  6.5 177.0 %all-gather.7.cloned.1.call-start = ((), (), s32[]{:S(2)}) async-start(), calls=%async_computation.7 | async-start | bytes 2129920 | tf_op jit(solution)/shard_map/all_gather | solution.py:47
  7.3 176.4 %all-gather.9.cloned.1.call-start = ((), (), s32[]{:S(2)}) async-start(), calls=%async_computation.8 | async-start | bytes 2359296 | tf_op jit(solution)/shard_map/all_gather | solution.py:67
  8.0 179.8 %all-gather.13.cloned.1.call-start = ((), (), s32[]{:S(2)}) async-start(), calls=%async_computation.10 | async-start | bytes 2359296 | tf_op jit(solution)/shard_map/all_gather | solution.py:68
  25.4 52.2 %copy-start.2 = (bf16[256,512]{1,0:T(8,128)(2,1)S(1)}, bf16[256,512]{1,0:T(8,128)(2,1)}, u32[]{:S(2)}) copy-start(bf16[256,512]{1,0:T(8,128)(2,1)} %param.14) | copy-start | bytes 786436
  27.5 69.6 %copy-start.3 = (bf16[256,512]{1,0:T(8,128)(2,1)S(1)}, bf16[256,512]{1,0:T(8,128)(2,1)}, u32[]{:S(2)}) copy-start(bf16[256,512]{1,0:T(8,128)(2,1)} %param.16) | copy-start | bytes 786436
  28.7 86.5 %copy-start.5 = (s32[128]{0:T(128)S(1)}, s32[128]{0:T(128)}, u32[]{:S(2)}) copy-start(s32[128]{0:T(128)} %param.17) | copy-start | bytes 1540
  67.1 23.1 %all-to-all-start = ((bf16[64,256,8]{1,2,0:T(8,128)(2,1)}), bf16[64,256,8]{1,2,0:T(8,128)(2,1)S(1)}, u32[]{:S(2)}, u32[]{:S(2)}) async-start(bf16[64,256,8]{1,2,0:T(8,128)(2,1)} %constant_dynamic-update-slice_fusion), calls=%async_computation | async-start | bytes 524288 | tf_op jit(solution)/shard_map/all_to_all | solution.py:13
  90.2 18.6 %all-to-all-start.2 = ((bf16[256,64,8]{0,2,1:T(8,128)(2,1)}), bf16[256,64,8]{0,2,1:T(8,128)(2,1)S(1)}, u32[]{:S(2)}, u32[]{:S(2)}) async-start(bf16[256,64,8]{0,2,1:T(8,128)(2,1)} %bitcast.69), calls=%async_computation.2 | async-start | bytes 524288 | tf_op jit(solution)/shard_map/all_to_all | solution.py:51
  108.8 18.0 %all-to-all-start.4 = ((bf16[256,64,8]{0,2,1:T(8,128)(2,1)}), bf16[256,64,8]{0,2,1:T(8,128)(2,1)S(1)}, u32[]{:S(2)}, u32[]{:S(2)}) async-start(bf16[256,64,8]{0,2,1:T(8,128)(2,1)} %bitcast.76), calls=%async_computation.4 | async-start | bytes 524288 | tf_op jit(solution)/shard_map/all_to_all | solution.py:52
  115.2 117.9 %all-gather.11.cloned.1.call-start = ((), (), s32[]{:S(2)}) async-start(), calls=%async_computation.9 | async-start | bytes 2359296 | tf_op jit(solution)/shard_map/all_gather | solution.py:69
  127.6 43.3 %copy-start.4 = (bf16[256,512]{1,0:T(8,128)(2,1)S(1)}, bf16[256,512]{1,0:T(8,128)(2,1)}, u32[]{:S(2)}) copy-start(bf16[256,512]{1,0:T(8,128)(2,1)} %param.15) | copy-start | bytes 786436
  146.4 131.3 %all-gather.15.cloned.1.call-start = ((), (), s32[]{:S(2)}) async-start(), calls=%async_computation.11 | async-start | bytes 2359296 | tf_op jit(solution)/shard_map/all_gather | solution.py:70
  164.5 18.0 %all-to-all-start.5 = ((bf16[64,256,8]{1,2,0:T(8,128)(2,1)}), bf16[64,256,8]{1,2,0:T(8,128)(2,1)S(1)}, u32[]{:S(2)}, u32[]{:S(2)}) async-start(bf16[64,256,8]{1,2,0:T(8,128)(2,1)} %bitcast.79), calls=%async_computation.5 | async-start | bytes 524288 | tf_op jit(solution)/shard_map/all_to_all | solution.py:61
  170.8 151.2 %all-gather.17.cloned.1.call-start = ((), (), s32[]{:S(2)}) async-start(), calls=%async_computation.12 | async-start | bytes 2359296 | tf_op jit(solution)/shard_map/all_gather | solution.py:102
  183.3 293.6 %reduce-scatter.2.cloned.1.call-start = ((), (), s32[]{:S(2)}) async-start(), calls=%async_computation.13 | async-start | bytes 4259840 | tf_op jit(solution)/shard_map/reduce_scatter | solution.py:105
  183.6 4.3 copy-start.1
Sparse Core Ops, SparseCore 0:
  10.7 87.8 all-gather.6
  100.7 42.7 all-gather.8
  145.6 42.2 all-gather.12
  189.8 43.2 all-gather.10
  235.0 42.7 all-gather.14
  279.7 42.3 all-gather.16
  326.7 150.1 reduce-scatter.1
